TPU v7x, 32 devices: a whole 2x2x4 slice. The times are simulated.
32 devices in a mesh: slides: 2 (over y), seq: 16 (over z, x, core), mp: 1.
Axes of the slice: x: 2, y: 2, z: 4, core: 2. Of those that a mesh axis runs over, the one named last changes fastest.
Arguments:
- tokens: bfloat16 [32768, 768], P(('slides', 'seq', 'mp')), parts along dimension 0, may hold values from -6 to 6
- attn_gain: float32 [768], replicated, may hold values from 0.25 to 1.75
- query_first: bfloat16 [768, 768], P(None, 'mp'), may hold values from -4 to 4
- key_first: bfloat16 [768, 768], P(None, 'mp'), may hold values from -4 to 4
- segment_value: bfloat16 [768, 768], P(None, 'mp'), may hold values from -0.21875 to 0.21875
- output_first: bfloat16 [768, 768], P('mp'), may hold values from -0.875 to 0.875
- mlp_gain: float32 [768], replicated, may hold values from 0.25 to 1.75
- up_weight: bfloat16 [768, 3072], P(None, 'mp'), may hold values from -0.21875 to 0.21875
- down_weight: bfloat16 [3072, 768], P('mp'), may hold values from -0.109375 to 0.109375
- second_gain: float32 [768], replicated, may hold values from 0.25 to 1.75
- query_second: bfloat16 [768, 768], P(None, 'mp'), may hold values from -4 to 4
- key_second: bfloat16 [768, 768], P(None, 'mp'), may hold values from -4 to 4
- value_second: bfloat16 [768, 768], P(None, 'mp'), may hold values from -0.21875 to 0.21875
- output_second: bfloat16 [768, 768], P('mp'), may hold values from -0.875 to 0.875
- segment_offset: int32 [16], P('mp'), may hold values from 0 to 63
- global_offset: int32 [16], P('mp'), may hold values from 0 to 63
Outputs:
- encoded: bfloat16 [32768, 768], P(('slides', 'seq', 'mp')), parts along dimension 0
There are 2 independent parts, one for each index of `slides`. A program takes and returns all parts, laid end to end along the dimension named above; an argument that names none is the same for every part. Nothing has to cross between parts.
All inputs are finite; a program needn't handle non-finite values.
Results may differ from a plain program's by a relative error of at most 0.03.
The roundings to bfloat16 on the way count: a program that leaves them out, or rounds other values in their place, can miss the bound.
Values may be sent and summed in bfloat16 or wider, within the bound.
A program may use at most 128 MiB of HBM per device.

v0:
```python
import jax
import jax.numpy as jnp
from jax import lax
from jax.sharding import PartitionSpec as P

KEYS = 256
SEG_MAX = 16


def swapped(x, axis, apart):
    return lax.ppermute(x, axis, [(i, i ^ 1 << apart) for i in range(lax.axis_size(axis))])


def norm_rows(values, gain):
    center = values - jnp.mean(values, axis=-1, keepdims=True)
    spread = jnp.mean(center * center, axis=-1, keepdims=True)
    return (center * lax.rsqrt(spread + 1e-05) * gain).astype(jnp.bfloat16)


def pick_keys(hidden, offsets, stride, key_weight, value_weight):
    token_count, width = hidden.shape
    head_count = offsets.shape[0]
    head_size = key_weight.shape[1] // head_count
    grouped_rows = hidden.reshape(token_count // stride, stride, width)
    dilation_selector = (
        lax.broadcasted_iota(jnp.int32, (stride, head_count), 0) == offsets[None, :]
    ).astype(jnp.bfloat16)
    chosen = jnp.einsum(
        "nof,oj->njf", grouped_rows, dilation_selector, preferred_element_type=jnp.float32
    ).astype(jnp.bfloat16)
    key_heads = jnp.einsum(
        "xkr,rkf->xkf",
        chosen,
        key_weight.reshape(width, head_count, head_size),
        preferred_element_type=jnp.float32,
    ).astype(jnp.bfloat16)
    value_heads = jnp.einsum(
        "xkr,rkf->xkf",
        chosen,
        value_weight.reshape(width, head_count, head_size),
        preferred_element_type=jnp.float32,
    ).astype(jnp.bfloat16)
    picked = token_count // stride
    return jnp.stack(
        [
            key_heads.reshape(picked, head_count * head_size),
            value_heads.reshape(picked, head_count * head_size),
        ]
    )


def attend_local(query, keyval, head_count):
    token_count, width = query.shape
    head_size = width // head_count
    query_heads = query.reshape(token_count, head_count, head_size)
    key_heads = keyval[0].reshape(-1, head_count, head_size)
    value_heads = keyval[1].reshape(-1, head_count, head_size)
    scores = jnp.einsum(
        "thd,khd->htk", query_heads, key_heads, preferred_element_type=jnp.float32
    ) * head_size ** (-0.5)
    highest = jnp.max(scores, axis=-1, keepdims=True)
    weights = jnp.exp(scores - highest)
    weights = (weights / jnp.sum(weights, axis=-1, keepdims=True)).astype(jnp.bfloat16)
    mixed = jnp.einsum(
        "htk,khd->thd", weights, value_heads, preferred_element_type=jnp.float32
    ).astype(jnp.bfloat16)
    return mixed.reshape(token_count, width)


def merge_branch_pair(mine, other, level, token_position):
    lower = token_position >> level & 1 == 0
    return jnp.where(
        lower, jnp.concatenate((mine, other), axis=1), jnp.concatenate((other, mine), axis=1)
    )


def spread_segment(keyval, seg_span, token_position):
    for level in range(seg_span.bit_length() - 1):
        partner = swapped(keyval, "seq", level)
        keyval = merge_branch_pair(keyval, partner, level, token_position)
    return keyval


def spread_global(keyval_two):
    keyval_two = lax.all_gather(keyval_two, "seq", axis=1, tiled=True)
    return keyval_two


def combine(partial_value, residual_full, need_full):
    row_count = residual_full.shape[0] // lax.axis_size("mp")
    row_start = lax.axis_index("mp") * row_count
    share = lax.psum_scatter(partial_value, "mp", scatter_dimension=0, tiled=True)
    own_rows = lax.dynamic_slice_in_dim(residual_full, row_start, row_count, 0)
    own_rows = (own_rows.astype(jnp.float32) + share).astype(jnp.bfloat16)
    full_rows = lax.all_gather(own_rows, "mp", axis=0, tiled=True) if need_full else own_rows
    return (own_rows, full_rows)


def body(
    tokens,
    attn_gain,
    query_first,
    key_first,
    segment_value,
    output_first,
    mlp_gain,
    up_weight,
    down_weight,
    second_gain,
    query_second,
    key_second,
    value_second,
    output_second,
    segment_offset,
    global_offset,
):
    seq_count = lax.axis_size("seq")
    token_position = lax.axis_index("seq")
    seg_span = min(SEG_MAX, seq_count)
    head_count = segment_offset.shape[0]
    full_rows = lax.all_gather(tokens, "mp", axis=0, tiled=True)
    token_count = full_rows.shape[0]
    hidden = norm_rows(full_rows.astype(jnp.float32), attn_gain)
    query = jnp.dot(hidden, query_first, preferred_element_type=jnp.float32).astype(jnp.bfloat16)
    seg_stride = token_count // (KEYS // seg_span)
    keyval = pick_keys(hidden, segment_offset, seg_stride, key_first, segment_value)
    keyval = spread_segment(keyval, seg_span, token_position)
    mixed = attend_local(query, keyval, head_count)
    partial_value = jnp.dot(mixed, output_first, preferred_element_type=jnp.float32)
    own_rows, first_rows = combine(partial_value, full_rows, True)
    normed = norm_rows(first_rows.astype(jnp.float32), mlp_gain)
    inner = jax.nn.gelu(
        jnp.dot(normed, up_weight, preferred_element_type=jnp.float32), approximate=True
    ).astype(jnp.bfloat16)
    partial_value = jnp.dot(inner, down_weight, preferred_element_type=jnp.float32)
    own_rows, second_rows = combine(partial_value, first_rows, True)
    hidden_two = norm_rows(second_rows.astype(jnp.float32), second_gain)
    query_two = jnp.dot(hidden_two, query_second, preferred_element_type=jnp.float32).astype(
        jnp.bfloat16
    )
    glob_stride = token_count // (KEYS // seq_count)
    keyval_two = pick_keys(hidden_two, global_offset, glob_stride, key_second, value_second)
    keyval_two = spread_global(keyval_two)
    mixed_two = attend_local(query_two, keyval_two, head_count)
    partial_value = jnp.dot(mixed_two, output_second, preferred_element_type=jnp.float32)
    own_rows, unused_rows = combine(partial_value, second_rows, False)
    return own_rows


def solution(mesh):
    placed = (
        P(("slides", "seq", "mp"), None),
        P(),
        P(None, "mp"),
        P(None, "mp"),
        P(None, "mp"),
        P("mp", None),
        P(),
        P(None, "mp"),
        P("mp", None),
        P(),
        P(None, "mp"),
        P(None, "mp"),
        P(None, "mp"),
        P("mp", None),
        P("mp"),
        P("mp"),
    )
    return jax.shard_map(
        body,
        mesh=mesh,
        in_specs=placed,
        out_specs=P(("slides", "seq", "mp"), None),
        check_vma=False,
    )
```

profile of v0, /device:TPU:0, one launch (start us, length us, event | category | flops | bytes accessed | tf_op | source)
XLA Modules:
  0.0 132.9 jit_solution(15052510869012871012)
XLA Ops:
  0.0 2.5 %copy.27 = bf16[768,768]{0,1:T(8,128)(2,1)} copy(bf16[768,768]{1,0:T(8,128)(2,1)} %param.19) | data formatting | bytes 2359296 | tf_op args[3]
  2.8 0.6 fusion.34
  3.5 0.5 fusion.36
  4.0 1.1 copy-done.3
  6.1 2.4 %copy.30 = bf16[768,768]{0,1:T(8,128)(2,1)} copy(bf16[768,768]{1,0:T(8,128)(2,1)} %param.20) | data formatting | bytes 2359296 | tf_op args[4]
  8.5 1.7 %fusion.63 = bf16[16,16,48]{2,0,1:T(8,128)(2,1)S(1)} fusion(bf16[768,16,48]{0,2,1:T(8,128)(2,1)} %bitcast.67, bf16[16,16,768]{2,1,0:T(8,128)(2,1)S(1)} %fusion.60), kind=kOutput, calls=%fused_computation.70 | convolution fusion | flops 18886656 | bytes 1597440 | tf_op jit(solution)/shard_map/xkr,rkf->xkf/dot_general | solution.py:37
  10.3 0.6 collective-permute-start
  10.9 0.9 collective-permute-done
  11.8 2.9 %collective-permute-start.1 = (bf16[2,32,768]{2,1,0:T(8,128)(2,1)S(1)}, bf16[2,32,768]{2,1,0:T(8,128)(2,1)S(1)}, u32[]{:S(2)}, u32[]{:S(2)}) collective-permute-start(bf16[2,32,768]{2,1,0:T(8,128)(2,1)S(1)} %maximum_select_fusion.3), channel_id=1, source_target_pairs={{0,2},{1,3},{2,0},{3,1},{4,6},{5,7},{6,4},{7,5},{8,10},{9,11},{10,... | collective-permute-start | bytes 294920 | tf_op jit(solution)/shard_map/ppermute | solution.py:11
  14.7 3.1 %collective-permute-done.1 = bf16[2,32,768]{2,1,0:T(8,128)(2,1)S(1)} collective-permute-done((bf16[2,32,768]{2,1,0:T(8,128)(2,1)S(1)}, bf16[2,32,768]{2,1,0:T(8,128)(2,1)S(1)}, u32[]{:S(2)}, u32[]{:S(2)}) %collective-permute-start.1) | collective-permute-done | bytes 98336 | tf_op jit(solution)/shard_map/ppermute | solution.py:11
  17.9 1.9 %collective-permute-start.2 = (bf16[2,64,768]{2,1,0:T(8,128)(2,1)S(1)}, bf16[2,64,768]{2,1,0:T(8,128)(2,1)S(1)}, u32[]{:S(2)}, u32[]{:S(2)}) collective-permute-start(bf16[2,64,768]{2,1,0:T(8,128)(2,1)S(1)} %maximum_select_fusion.2), channel_id=1, source_target_pairs={{0,4},{1,5},{2,6},{3,7},{4,0},{5,1},{6,2},{7,3},{8,12},{9,13},{10,... | collective-permute-start | bytes 589832 | tf_op jit(solution)/shard_map/ppermute | solution.py:11
  19.8 4.6 %collective-permute-done.2 = bf16[2,64,768]{2,1,0:T(8,128)(2,1)S(1)} collective-permute-done((bf16[2,64,768]{2,1,0:T(8,128)(2,1)S(1)}, bf16[2,64,768]{2,1,0:T(8,128)(2,1)S(1)}, u32[]{:S(2)}, u32[]{:S(2)}) %collective-permute-start.2) | collective-permute-done | bytes 196640 | tf_op jit(solution)/shard_map/ppermute | solution.py:11
  24.4 2.6 %collective-permute-start.3 = (bf16[2,128,768]{2,1,0:T(8,128)(2,1)S(1)}, bf16[2,128,768]{2,1,0:T(8,128)(2,1)S(1)}, u32[]{:S(2)}, u32[]{:S(2)}) collective-permute-start(bf16[2,128,768]{2,1,0:T(8,128)(2,1)S(1)} %maximum_select_fusion.1), channel_id=1, source_target_pairs={{0,8},{1,9},{2,10},{3,11},{4,12},{5,13},{6,14},{7,15},{8,0},{9,1},... | collective-permute-start | bytes 1179656 | tf_op jit(solution)/shard_map/ppermute | solution.py:11
  27.0 2.4 %copy.39 = bf16[768,768]{0,1:T(8,128)(2,1)} copy(bf16[768,768]{1,0:T(8,128)(2,1)} %param.28) | data formatting | bytes 2359296 | tf_op args[12]
  29.4 2.4 %copy.36 = bf16[768,768]{0,1:T(8,128)(2,1)} copy(bf16[768,768]{1,0:T(8,128)(2,1)} %param.27) | data formatting | bytes 2359296 | tf_op args[11]
  31.8 4.3 %convolution_convert_fusion.1 = bf16[1024,768]{0,1:T(8,128)(2,1)} fusion(bf16[1024,768]{1,0:T(8,128)(2,1)} %copy-done.3, bf16[768,768]{1,0:T(8,128)(2,1)} %param.18), kind=kOutput, calls=%fused_computation.57 | convolution fusion | flops 1208745984 | bytes 4325376 | tf_op jit(solution)/shard_map/dot_general | solution.py:124
  36.1 7.4 %collective-permute-done.3 = bf16[2,128,768]{2,1,0:T(8,128)(2,1)S(1)} collective-permute-done((bf16[2,128,768]{2,1,0:T(8,128)(2,1)S(1)}, bf16[2,128,768]{2,1,0:T(8,128)(2,1)S(1)}, u32[]{:S(2)}, u32[]{:S(2)}) %collective-permute-start.3) | collective-permute-done | bytes 393248 | tf_op jit(solution)/shard_map/ppermute | solution.py:11
  43.9 0.9 copy.33
  45.0 10.4 %fusion.84 = (f32[16,1024]{1,0:T(8,128)}, f32[16,1024,256]{1,2,0:T(8,128)}) fusion(bf16[1024,16,48]{0,2,1:T(8,128)(2,1)} %bitcast.72, bf16[256,16,48]{0,2,1:T(8,128)(2,1)S(1)} %bitcast.70), kind=kOutput, calls=%fused_computation.104 | convolution fusion | flops 415236352 | bytes 18808832 | tf_op jit(solution)/shard_map/sub | solution.py:62
  55.4 7.3 %fusion.47 = bf16[16,48,1024]{2,1,0:T(8,128)(2,1)S(1)} fusion(bf16[256,16,48]{0,2,1:T(8,128)(2,1)S(1)} %bitcast.69, f32[16,1024,256]{1,2,0:T(8,128)} %get-tuple-element.10, f32[16,1024]{1,0:T(8,128)} %get-tuple-element.9), kind=kOutput, calls=%fused_computation.55 | convolution fusion | flops 411828224 | bytes 18808832 | tf_op jit(solution)/shard_map/htk,khd->thd/dot_general | solution.py:64
  62.8 1.6 %convert_reduce_fusion.1 = (f32[1024]{0:T(1024)S(1)}, bf16[1024,768]{1,0:T(8,128)(2,1)S(1)}) fusion(bf16[1024,768]{0,1:T(8,128)(2,1)S(1)} %bitcast.74, bf16[768,768]{1,0:T(8,128)(2,1)S(1)} %copy-done, bf16[1024,768]{1,0:T(8,128)(2,1)S(1)} %copy-done.2), kind=kOutput, calls=%fused_computation.29 | convolution fusion | flops 1211890688 | bytes 5902336 | tf_op jit(solution)/shard_map/dot_general | solution.py:129
  64.3 0.6 fusion.31
  65.0 0.5 copy-done.8
  65.5 15.5 %convert_reduce_fusion = (f32[1024]{0:T(1024)S(1)}, bf16[1024,768]{1,0:T(8,128)(2,1)S(1)}) fusion(bf16[3072,768]{1,0:T(8,128)(2,1)} %param.24, bf16[768,3072]{1,0:T(8,128)(2,1)} %param.23, bf16[1024,768]{1,0:T(8,128)(2,1)} %copy-done.8, f32[768]{0:T(1024)S(1)} %copy-done.15, f32[1024]{0:T(1024)S(1)} %add_rsqrt_fusion.1, f32[1024]{0:T(1024)S(1)} %broadcast_multiply_fusion.1), kind=kOutput, calls=%fused_computation.26 | convolution fusion | flops 9699851264 | bytes 12598272 | tf_op jit(solution)/shard_map/dot_general | solution.py:135
  81.0 0.6 fusion.28
  81.6 0.5 fusion.30
  82.2 1.1 copy-done.4
  84.9 23.6 %all_gather.2 = bf16[2,256,768]{2,1,0:T(8,128)(2,1)S(1)} all-gather(bf16[2,16,768]{2,1,0:T(8,128)(2,1)S(1)} %pad_maximum_fusion), channel_id=1, replica_groups=mesh['slides'=2,'seq'=16,'mp'=1] {'seq'}, dimensions={1}, use_global_device_ids=true | all-gather | bytes 835584 | tf_op jit(solution)/shard_map/all_gather | solution.py:85
  108.7 4.3 %convolution_convert_fusion = bf16[1024,768]{0,1:T(8,128)(2,1)} fusion(bf16[1024,768]{1,0:T(8,128)(2,1)} %copy-done.4, bf16[768,768]{1,0:T(8,128)(2,1)} %param.26), kind=kOutput, calls=%fused_computation.56 | convolution fusion | flops 1208745984 | bytes 4325376 | tf_op jit(solution)/shard_map/dot_general | solution.py:138
  113.2 9.7 %fusion.87 = (f32[16,1024]{1,0:T(8,128)S(1)}, f32[16,1024,256]{1,2,0:T(8,128)}) fusion(bf16[1024,16,48]{0,2,1:T(8,128)(2,1)} %bitcast.73, bf16[256,16,48]{0,2,1:T(8,128)(2,1)S(1)} %bitcast.71), kind=kOutput, calls=%fused_computation.105 | convolution fusion | flops 415236352 | bytes 18808832 | tf_op jit(solution)/shard_map/sub | solution.py:62
  122.9 7.4 %fusion.46 = bf16[16,48,1024]{2,1,0:T(8,128)(2,1)S(1)} fusion(bf16[256,16,48]{0,2,1:T(8,128)(2,1)S(1)} %bitcast.68, f32[16,1024,256]{1,2,0:T(8,128)} %get-tuple-element.16, f32[16,1024]{1,0:T(8,128)S(1)} %get-tuple-element.15), kind=kOutput, calls=%fused_computation.54 | convolution fusion | flops 411828224 | bytes 18808832 | tf_op jit(solution)/shard_map/htk,khd->thd/dot_general | solution.py:64
  130.4 2.6 %fusion.39 = bf16[1024,768]{1,0:T(8,128)(2,1)} fusion(bf16[1024,768]{1,0:T(8,128)(2,1)S(1)} %get-tuple-element.14, bf16[1024,768]{0,1:T(8,128)(2,1)S(1)} %bitcast.75, bf16[768,768]{1,0:T(8,128)(2,1)S(1)} %copy-done.14), kind=kOutput, calls=%fused_computation.50 | convolution fusion | flops 1210318848 | bytes 5898240 | tf_op jit(solution)/shard_map/dot_general | solution.py:145
  (61 shorter events, 4.0 us)
Async XLA Ops:
  0.0 62.7 %copy-start = (bf16[768,768]{1,0:T(8,128)(2,1)S(1)}, bf16[768,768]{1,0:T(8,128)(2,1)}, u32[]{:S(2)}) copy-start(bf16[768,768]{1,0:T(8,128)(2,1)} %param.21) | copy-start | bytes 3538948
  0.0 2.5 %copy-start.2 = (bf16[1024,768]{1,0:T(8,128)(2,1)S(1)}, bf16[1024,768]{1,0:T(8,128)(2,1)}, u32[]{:S(2)}) copy-start(bf16[1024,768]{1,0:T(8,128)(2,1)} %param.16) | copy-start | bytes 4718596
  0.0 3.4 %copy-start.10 = (f32[768]{0:T(1024)S(1)}, f32[768]{0:T(1024)}, u32[]{:S(2)}) copy-start(f32[768]{0:T(1024)} %param.17) | copy-start | bytes 9220
  2.5 2.6 %copy-start.12 = (s32[16]{0:T(128)S(1)}, s32[16]{0:T(128)}, u32[]{:S(2)}) copy-start(s32[16]{0:T(128)} %param.30) | copy-start | bytes 196
  2.8 2.7 %copy-start.7 = (bf16[768,768]{0,1:T(8,128)(2,1)S(1)}, bf16[768,768]{0,1:T(8,128)(2,1)}, u32[]{:S(2)}) copy-start(bf16[768,768]{0,1:T(8,128)(2,1)} %copy.27) | copy-start | bytes 3538948
  4.0 1.1 copy-start.3
  10.3 1.4 %collective-permute-start = (bf16[2,16,768]{2,1,0:T(8,128)(2,1)S(1)}, bf16[2,16,768]{2,1,0:T(8,128)(2,1)S(1)}, u32[]{:S(2)}, u32[]{:S(2)}) collective-permute-start(bf16[2,16,768]{2,1,0:T(8,128)(2,1)S(1)} %constant_dynamic-update-slice_fusion), channel_id=1, source_target_pairs={{0,1},{1,0},{2,3},{3,2},{4,5},{5,4},{6,7},{7,6},{8,9},{9,8},{10,11... | collective-permute-start | bytes 147464 | tf_op jit(solution)/shard_map/ppermute | solution.py:11
  11.8 6.0 %collective-permute-start.1 = (bf16[2,32,768]{2,1,0:T(8,128)(2,1)S(1)}, bf16[2,32,768]{2,1,0:T(8,128)(2,1)S(1)}, u32[]{:S(2)}, u32[]{:S(2)}) collective-permute-start(bf16[2,32,768]{2,1,0:T(8,128)(2,1)S(1)} %maximum_select_fusion.3), channel_id=1, source_target_pairs={{0,2},{1,3},{2,0},{3,1},{4,6},{5,7},{6,4},{7,5},{8,10},{9,11},{10,... | collective-permute-start | bytes 294920 | tf_op jit(solution)/shard_map/ppermute | solution.py:11
  17.9 6.5 %collective-permute-start.2 = (bf16[2,64,768]{2,1,0:T(8,128)(2,1)S(1)}, bf16[2,64,768]{2,1,0:T(8,128)(2,1)S(1)}, u32[]{:S(2)}, u32[]{:S(2)}) collective-permute-start(bf16[2,64,768]{2,1,0:T(8,128)(2,1)S(1)} %maximum_select_fusion.2), channel_id=1, source_target_pairs={{0,4},{1,5},{2,6},{3,7},{4,0},{5,1},{6,2},{7,3},{8,12},{9,13},{10,... | collective-permute-start | bytes 589832 | tf_op jit(solution)/shard_map/ppermute | solution.py:11
  24.4 19.1 %collective-permute-start.3 = (bf16[2,128,768]{2,1,0:T(8,128)(2,1)S(1)}, bf16[2,128,768]{2,1,0:T(8,128)(2,1)S(1)}, u32[]{:S(2)}, u32[]{:S(2)}) collective-permute-start(bf16[2,128,768]{2,1,0:T(8,128)(2,1)S(1)} %maximum_select_fusion.1), channel_id=1, source_target_pairs={{0,8},{1,9},{2,10},{3,11},{4,12},{5,13},{6,14},{7,15},{8,0},{9,1},... | collective-permute-start | bytes 1179656 | tf_op jit(solution)/shard_map/ppermute | solution.py:11
  45.0 10.4 %copy-start.9 = (bf16[1,256,768]{1,2,0:T(8,128)(2,1)S(1)}, bf16[1,256,768]{1,2,0:T(8,128)(2,1)}, u32[]{:S(2)}) copy-start(bf16[1,256,768]{1,2,0:T(8,128)(2,1)} %copy.33) | copy-start | bytes 1179652
  62.7 2.7 %copy-start.15 = (f32[768]{0:T(1024)S(1)}, f32[768]{0:T(1024)}, u32[]{:S(2)}) copy-start(f32[768]{0:T(1024)} %param.22) | copy-start | bytes 9220
  64.3 1.1 copy-start.8
  65.5 16.1 %copy-start.11 = (f32[768]{0:T(1024)S(1)}, f32[768]{0:T(1024)}, u32[]{:S(2)}) copy-start(f32[768]{0:T(1024)} %param.25) | copy-start | bytes 9220
  81.0 2.4 %copy-start.13 = (s32[16]{0:T(128)S(1)}, s32[16]{0:T(128)}, u32[]{:S(2)}) copy-start(s32[16]{0:T(128)} %param.31) | copy-start | bytes 196
  81.0 2.7 %copy-start.6 = (bf16[768,768]{0,1:T(8,128)(2,1)S(1)}, bf16[768,768]{0,1:T(8,128)(2,1)}, u32[]{:S(2)}) copy-start(bf16[768,768]{0,1:T(8,128)(2,1)} %copy.39) | copy-start | bytes 3538948
  81.6 2.7 %copy-start.5 = (bf16[768,768]{0,1:T(8,128)(2,1)S(1)}, bf16[768,768]{0,1:T(8,128)(2,1)}, u32[]{:S(2)}) copy-start(bf16[768,768]{0,1:T(8,128)(2,1)} %copy.36) | copy-start | bytes 3538948
  82.2 1.1 copy-start.4
  122.9 7.5 %copy-start.14 = (bf16[768,768]{1,0:T(8,128)(2,1)S(1)}, bf16[768,768]{1,0:T(8,128)(2,1)}, u32[]{:S(2)}) copy-start(bf16[768,768]{1,0:T(8,128)(2,1)} %param.29) | copy-start | bytes 3538948
  130.3 2.6 %copy-start.1 = (bf16[768,768]{1,0:T(8,128)(2,1)S(1)}, bf16[768,768]{1,0:T(8,128)(2,1)}, u32[]{:S(2)}) copy-start(bf16[768,768]{1,0:T(8,128)(2,1)} %param.21) | copy-start | bytes 3538948
where the time goes:
time: 133 us
  matrix products  66.8 us (50%)
  blocking collectives  23.6 us (18%)
  waiting for transfers between devices  16 us (12%)
  local copies, waits for them, and re-layouts  14.6 us (11%)
  starting transfers between devices  7.97 us (6%)
  other arithmetic  3.63 us (3%)
    all_gather x1, blocking collectives, spread_global(): keyval_two = lax.all_gather(keyval_two, 'seq', axis=1, tiled=True)  23.6 us
    sub x2, matrix products, attend_local(): weights = jnp.exp(scores - highest)  20.1 us
    ppermute x4, waiting for transfers between devices, swapped(): lax.ppermute(x, axis, [(i, i ^ 1 << apart) for i in range(lax.axis_size(a...  16 us
    dot_general x1, matrix products, body(): jnp.dot(inner, down_weight, preferred_element_type=jnp.float32)  15.5 us
    dot_general x2, matrix products, attend_local(): jnp.einsum('htk,khd->thd', weights, value_heads, preferred_element_type=j...  14.8 us
    unnamed x37, local copies, waits for them, and re-layouts  12.5 us
    ppermute x4, starting transfers between devices, swapped(): lax.ppermute(x, axis, [(i, i ^ 1 << apart) for i in range(lax.axis_size(a...  7.97 us
    dot_general x1, matrix products, body(): jnp.dot(hidden_two, query_second, preferred_element_type=jnp.float32)  4.34 us
  transfers between devices with their start and end apart: 4, of which 4 were waited for; matrix products, arithmetic and copies ran while one was open for 7% of the time, Pallas kernels for 0%

commit v1 on v0

--- a/solution.py
+++ b/solution.py
@@ -1,6 +1,11 @@
+import functools
+import math
+
 import jax
 import jax.numpy as jnp
 from jax import lax
+from jax.experimental import pallas as pl
+from jax.experimental.pallas import tpu as pltpu
 from jax.sharding import PartitionSpec as P
 
 KEYS = 256
@@ -147,6 +152,350 @@
     return own_rows
 
 
+MESH = pl.DeviceIdType.MESH
+F32 = jnp.float32
+BF16 = jnp.bfloat16
+WINDOW = 256
+LANES = 128
+
+
+def iota(shape, axis):
+    return lax.broadcasted_iota(jnp.int32, shape, axis)
+
+
+def dot32(a, b):
+    return jnp.dot(a, b, preferred_element_type=F32)
+
+
+def gelu(x):
+    return 0.5 * x * (1.0 + jnp.tanh(math.sqrt(2.0 / math.pi) * (x + 0.044715 * (x * x * x))))
+
+
+class Gather:
+    def __init__(self, n, buf, ssem, rsem):
+        me = lax.axis_index("seq")
+        self.me, self.n, self.high = me, n, n // 4
+        self.buf, self.ssem, self.rsem = buf, ssem, rsem
+        self.b0, self.b1, self.hi = me % 2, (me // 2) % 2, me // 4
+        self.peer1 = self.hi * 4 + (1 - self.b1) * 2 + self.b0
+        self.peer0 = self.hi * 4 + self.b1 * 2 + (1 - self.b0)
+
+    def slot(self, d, b1, b0):
+        return ((self.hi + self.high - d) % self.high) * 4 + b1 * 2 + b0
+
+    def copy(self, slot, peer, k):
+        return pltpu.make_async_remote_copy(
+            src_ref=self.buf.at[slot],
+            dst_ref=self.buf.at[slot],
+            send_sem=self.ssem.at[k],
+            recv_sem=self.rsem.at[slot],
+            device_id={"seq": peer},
+            device_id_type=MESH,
+        )
+
+    def peers(self):
+        out = [((self.hi + d) % self.high) * 4 + self.b1 * 2 + self.b0 for d in range(1, self.high)]
+        return out + [self.peer1, self.peer0]
+
+    def start(self):
+        h = self.high
+        for d in range(1, h):
+            peer = ((self.hi + d) % h) * 4 + self.b1 * 2 + self.b0
+            self.copy(self.me, peer, d - 1).start()
+        self.copy(self.me, self.peer1, h - 1).start()
+        self.copy(self.me, self.peer0, 2 * h - 1).start()
+
+    def second(self):
+        h = self.high
+        for d in range(1, h):
+            slot = self.slot(d, self.b1, self.b0)
+            self.copy(slot, self.peer1, h - 1 + d).wait_recv()
+            self.copy(slot, self.peer1, h - 1 + d).start()
+            self.copy(slot, self.peer0, 2 * h - 1 + d).start()
+
+    def third(self):
+        h = self.high
+        for d in range(h):
+            slot = self.slot(d, 1 - self.b1, self.b0)
+            self.copy(slot, self.peer0, 3 * h - 1 + d).wait_recv()
+            self.copy(slot, self.peer0, 3 * h - 1 + d).start()
+
+    def finish(self):
+        h = self.high
+        for b1 in (self.b1, 1 - self.b1):
+            for d in range(h):
+                slot = self.slot(d, b1, 1 - self.b0)
+                self.copy(slot, self.peer0, 0).wait_recv()
+        for k in range(4 * h - 1):
+            self.copy(self.me, self.peer0, k).wait_send()
+
+
+def head_column(offset_ref, heads, picked):
+    rows = iota((heads * picked, 1), 0) // picked
+    column = jnp.zeros((heads * picked, 1), jnp.int32)
+    for h in range(heads):
+        column = jnp.where(rows == h, offset_ref[h], column)
+    return column
+
+
+def kernel(
+    n, heads, picked, stride,
+    seg_ref, glob_ref, x_ref, gain1_ref, gain_mlp_ref, gain2_ref,
+    wq1_hbm, wk1_hbm, wv1_hbm, wo1_hbm, up_hbm, down_hbm, wq2_hbm, wk2_hbm, wv2_hbm, wo2_hbm,
+    out_ref,
+    wq1, wk1, wv1, wo1, up, down, wq2, wk2, wv2, wo2, wo_pad1, wo_pad2,
+    xp, q, kv1, kv2, km, vp, perm, perm_back, mix, inner, sem, ssem1, rsem1, ssem2, rsem2,
+):
+    tokens, width = x_ref.shape
+    size = width // heads
+    half = LANES // 2
+    chunk = heads * picked
+    chunks = tokens // chunk
+    keys = n * picked
+    group = WINDOW // stride
+    scale = size ** -0.5 * math.log2(math.e)
+
+    pairs = [(wk1_hbm, wk1), (wv1_hbm, wv1), (wq1_hbm, wq1), (wo1_hbm, wo1), (up_hbm, up),
+             (down_hbm, down), (wk2_hbm, wk2), (wv2_hbm, wv2), (wq2_hbm, wq2), (wo2_hbm, wo2)]
+    loads = [pltpu.make_async_copy(a, b, sem.at[i]) for i, (a, b) in enumerate(pairs)]
+    for load in loads:
+        load.start()
+
+    first_gather = Gather(n, kv1, ssem1, rsem1)
+    second_gather = Gather(n, kv2, ssem2, rsem2)
+    barrier = pltpu.get_barrier_semaphore()
+    peers = first_gather.peers()
+    for peer in peers:
+        pl.semaphore_signal(barrier, inc=1, device_id={"seq": peer}, device_id_type=MESH)
+
+    def own_heads(hidden, weight):
+        full = dot32(hidden, weight[...])
+        column = iota((picked, width), 1)
+        total = jnp.zeros((picked, width), F32)
+        for h in range(heads):
+            mine = (column >= h * size) & (column < h * size + size)
+            total = jnp.where(mine, full[h * picked:(h + 1) * picked], total)
+        return total.astype(BF16)
+
+    rows = iota((chunk, 1), 0)
+    pick = rows % picked
+    target = pick * stride + head_column(seg_ref, heads, picked)
+    onehot = (iota((chunk, tokens), 1) == target).astype(F32).astype(BF16)
+    hidden = norm_rows(dot32(onehot, x_ref[...]), gain1_ref[...])
+    me = first_gather.me
+    loads[0].wait()
+    kv1[me, 0:picked, :] = own_heads(hidden, wk1)
+    loads[1].wait()
+    kv1[me, picked:2 * picked, :] = own_heads(hidden, wv1)
+    pl.semaphore_wait(barrier, len(peers))
+    first_gather.start()
+
+    glob_col = head_column(glob_ref, heads, picked)
+    lane = iota((16, WINDOW), 1)
+    inside = lane % stride
+    chosen = jnp.zeros((16, WINDOW), F32)
+    for h in range(heads):
+        chosen = jnp.where(inside == glob_ref[h], 1.0, chosen)
+    a, b = iota((WINDOW, WINDOW), 0), iota((WINDOW, WINDOW), 1)
+    same = a // stride == b // stride
+    before = jnp.where(same & (a < b), 1.0, 0.0).astype(BF16)
+    count = dot32(chosen.astype(BF16), before)
+    total = dot32(chosen.astype(BF16), jnp.where(same, 1.0, 0.0).astype(BF16))
+    rank = jnp.where(chosen > 0.5, count, total + inside.astype(F32) - count)
+    rank_row = rank[0:1, :]
+    table = jnp.where(same & (rank_row == (a % stride).astype(F32)), 1.0, 0.0)
+    perm[...] = table.astype(BF16)
+    perm_back[...] = table.T.astype(BF16)
+    at_head = (iota((chunk, WINDOW), 1) == glob_col)
+    head_rank = jnp.sum(jnp.where(at_head, rank_row, 0.0), axis=1, keepdims=True)
+    spot = (pick * heads).astype(F32) + head_rank
+    onehot_two = (iota((chunk, chunk), 1).astype(F32) == spot).astype(F32).astype(BF16)
+
+    for g in range(tokens // WINDOW):
+        moved = dot32(perm[...], x_ref[g * WINDOW:(g + 1) * WINDOW, :]).astype(BF16)
+        for j in range(group):
+            for c in range(chunks):
+                at = c * chunk + (g * group + j) * heads
+                xp[at:at + heads, :] = moved[j * stride + c * heads:j * stride + (c + 1) * heads]
+
+    def window_of(h):
+        return min(h * size // LANES * LANES, width - WINDOW)
+
+    for h in range(heads):
+        km[h] = jnp.zeros((WINDOW, keys), BF16)
+        i = h % 2
+        ones = iota((keys, LANES), 1) // half == i
+        vp[h // 2, i * keys:(i + 1) * keys, LANES:] = jnp.where(ones, 1.0, 0.0).astype(BF16)
+    for source, padded, load in ((wo1, wo_pad1, loads[3]), (wo2, wo_pad2, None)):
+        if load is None:
+            continue
+        load.wait()
+        for h in range(heads):
+            padded[h * half:h * half + size, :] = source[h * size:(h + 1) * size, :]
+            padded[h * half + size:(h + 1) * half, :] = jnp.zeros((half - size, width), BF16)
+
+    first_gather.second()
+
+    loads[2].wait()
+
+    def query_chunk(c, carry):
+        at = pl.ds(pl.multiple_of(c * chunk, chunk), chunk)
+        hidden = norm_rows(xp[at, :].astype(F32), gain1_ref[...])
+        q[at, :] = dot32(hidden, wq1[...]).astype(BF16)
+        return carry
+
+    lax.fori_loop(0, chunks, query_chunk, 0)
+    first_gather.third()
+    first_gather.finish()
+
+    def set_keys(kv):
+        key = kv[:, 0:picked, :].reshape(keys, width)
+        value = kv[:, picked:2 * picked, :].reshape(keys, width)
+        turned = key.astype(F32).T.astype(BF16)
+        for h in range(heads):
+            begin = h * size - window_of(h)
+            km[h, begin:begin + size, :] = turned[h * size:(h + 1) * size, :]
+            i = h % 2
+            c, l = iota((WINDOW, LANES), 0) - begin, iota((WINDOW, LANES), 1) - i * half
+            shift = jnp.where((c == l) & (l >= 0) & (l < size), 1.0, 0.0).astype(BF16)
+            moved = dot32(value[:, window_of(h):window_of(h) + WINDOW], shift)
+            vp[h // 2, i * keys:(i + 1) * keys, 0:LANES] = moved.astype(BF16)
+
+    def attend(at):
+        for pair in range(heads // 2):
+            parts = []
+            for h in (2 * pair, 2 * pair + 1):
+                start = window_of(h)
+                scores = dot32(q[at, start:start + WINDOW], km[h])
+                top = jnp.max(scores, axis=-1, keepdims=True)
+                parts.append(jnp.exp2((scores - top) * scale).astype(BF16))
+            both = dot32(jnp.concatenate(parts, axis=1), vp[pair])
+            mixed = both[:, :LANES] / both[:, LANES:]
+            mix[:, pair * LANES:(pair + 1) * LANES] = mixed.astype(BF16)
+
+    set_keys(kv1)
+    loads[4].wait()
+    loads[5].wait()
+    loads[6].wait()
+    loads[7].wait()
+    loads[8].wait()
+
+    def first_chunk(c, carry):
+        at = pl.ds(pl.multiple_of(c * chunk, chunk), chunk)
+        attend(at)
+        first = (xp[at, :].astype(F32) + dot32(mix[...], wo_pad1[...])).astype(BF16)
+        normed = norm_rows(first.astype(F32), gain_mlp_ref[...])
+        hidden_units = up.shape[1]
+        for start in range(0, hidden_units, width):
+            part = dot32(normed, up[:, start:start + width])
+            inner[:, start:start + width] = gelu(part).astype(BF16)
+        second = (first.astype(F32) + dot32(inner[...], down[...])).astype(BF16)
+        xp[at, :] = second
+        hidden_two = norm_rows(second.astype(F32), gain2_ref[...])
+        q[at, :] = dot32(hidden_two, wq2[...]).astype(BF16)
+
+        @pl.when(c == 0)
+        def _():
+            picked_rows = dot32(onehot_two, hidden_two).astype(BF16)
+            kv2[me, 0:picked, :] = own_heads(picked_rows, wk2)
+            kv2[me, picked:2 * picked, :] = own_heads(picked_rows, wv2)
+            second_gather.start()
+
+        @pl.when(c == 1)
+        def _():
+            second_gather.second()
+
+        @pl.when(c == 2)
+        def _():
+            second_gather.third()
+
+        return carry
+
+    lax.fori_loop(0, chunks, first_chunk, 0)
+    loads[9].wait()
+    for h in range(heads):
+        wo_pad2[h * half:h * half + size, :] = wo2[h * size:(h + 1) * size, :]
+        wo_pad2[h * half + size:(h + 1) * half, :] = jnp.zeros((half - size, width), BF16)
+    second_gather.finish()
+    set_keys(kv2)
+
+    def last_chunk(c, carry):
+        at = pl.ds(pl.multiple_of(c * chunk, chunk), chunk)
+        attend(at)
+        xp[at, :] = (xp[at, :].astype(F32) + dot32(mix[...], wo_pad2[...])).astype(BF16)
+        return carry
+
+    lax.fori_loop(0, chunks, last_chunk, 0)
+    for g in range(tokens // WINDOW):
+        blocks = []
+        for j in range(group):
+            for c in range(chunks):
+                at = c * chunk + (g * group + j) * heads
+                blocks.append(xp[at:at + heads, :])
+        moved = dot32(perm_back[...], jnp.concatenate(blocks, axis=0))
+        out_ref[g * WINDOW:(g + 1) * WINDOW, :] = moved.astype(BF16)
+
+
+def whole_body(
+    tokens, attn_gain, query_first, key_first, segment_value, output_first, mlp_gain, up_weight,
+    down_weight, second_gain, query_second, key_second, value_second, output_second,
+    segment_offset, global_offset,
+):
+    n = lax.axis_size("seq")
+    heads = segment_offset.shape[0]
+    picked = KEYS // n
+    count, width = tokens.shape
+    stride = count // picked
+    units = up_weight.shape[1]
+    chunk = heads * picked
+    any_space = pl.BlockSpec(memory_space=pl.ANY)
+    vmem = pl.BlockSpec(memory_space=pltpu.VMEM)
+    smem = pl.BlockSpec(memory_space=pltpu.SMEM)
+    square = pltpu.VMEM((width, width), BF16)
+    padded = pltpu.VMEM((heads * LANES // 2, width), BF16)
+    return pl.pallas_call(
+        functools.partial(kernel, n, heads, picked, stride),
+        out_shape=jax.ShapeDtypeStruct(tokens.shape, tokens.dtype),
+        in_specs=[smem, smem, vmem, vmem, vmem, vmem] + [any_space] * 10,
+        out_specs=vmem,
+        scratch_shapes=[
+            square, square, square, square,
+            pltpu.VMEM((width, units), BF16), pltpu.VMEM((units, width), BF16),
+            square, square, square, square, padded, padded,
+            pltpu.VMEM((count, width), BF16),
+            pltpu.VMEM((count, width), BF16),
+            pltpu.VMEM((n, 2 * picked, width), BF16),
+            pltpu.VMEM((n, 2 * picked, width), BF16),
+            pltpu.VMEM((heads, WINDOW, KEYS), BF16),
+            pltpu.VMEM((heads // 2, 2 * KEYS, 2 * LANES), BF16),
+            pltpu.VMEM((WINDOW, WINDOW), BF16),
+            pltpu.VMEM((WINDOW, WINDOW), BF16),
+            pltpu.VMEM((chunk, heads * LANES // 2), BF16),
+            pltpu.VMEM((chunk, units), BF16),
+            pltpu.SemaphoreType.DMA((10,)),
+            pltpu.SemaphoreType.DMA((n,)), pltpu.SemaphoreType.DMA((n,)),
+            pltpu.SemaphoreType.DMA((n,)), pltpu.SemaphoreType.DMA((n,)),
+        ],
+        compiler_params=pltpu.CompilerParams(
+            collective_id=0, has_side_effects=True, vmem_limit_bytes=60 << 20
+        ),
+        name="encoder",
+    )(
+        segment_offset, global_offset, tokens, attn_gain[None], mlp_gain[None], second_gain[None],
+        query_first, key_first, segment_value, output_first, up_weight, down_weight,
+        query_second, key_second, value_second, output_second,
+    )
+
+
+def fits(mesh):
+    n = mesh.shape["seq"]
+    return mesh.shape["mp"] == 1 and n == SEG_MAX
+
+
+def choose(mesh):
+    return whole_body if fits(mesh) else body
+
+
 def solution(mesh):
     placed = (
         P(("slides", "seq", "mp"), None),
@@ -167,7 +516,7 @@
         P("mp"),
     )
     return jax.shard_map(
-        body,
+        choose(mesh),
         mesh=mesh,
         in_specs=placed,
         out_specs=P(("slides", "seq", "mp"), None),

time: 133 us -> 61 us (0.46)
  matrix products: 66.8 us -> 0 us
  Pallas kernels: 0 us -> 54.3 us
  blocking collectives: 23.6 us -> 0 us
  waiting for transfers between devices: 16 us -> 0 us
  local copies, waits for them, and re-layouts: 14.6 us -> 6.45 us
  starting transfers between devices: 7.97 us -> 0 us
  other arithmetic: 3.63 us -> 0 us
    pallas_call x0 -> x1, Pallas kernels: none -> 54.3 us  [whole_body(): pl.pallas_call(functools.partial(kernel, n, heads, picked, stride), out_s...]
    dot_general x13 -> x0, matrix products: 46.7 us -> none  [the longest x1 15.5 us: body(): jnp.dot(inner, down_weight, preferred_element_type=jnp.float32)]
    all_gather x1 -> x0, blocking collectives: 23.6 us -> none  [spread_global(): keyval_two = lax.all_gather(keyval_two, 'seq', axis=1, tiled=True)]
    sub x2 -> x0, matrix products: 20.1 us -> none  [attend_local(): weights = jnp.exp(scores - highest)]
    ppermute x4 -> x0, waiting for transfers between devices: 16 us -> none  [swapped(): lax.ppermute(x, axis, [(i, i ^ 1 << apart) for i in range(lax.axis_size(a...]
    unnamed x37 -> x1, local copies, waits for them, and re-layouts: 12.5 us -> 2.65 us
    ppermute x4 -> x0, starting transfers between devices: 7.97 us -> none  [swapped(): lax.ppermute(x, axis, [(i, i ^ 1 << apart) for i in range(lax.axis_size(a...]
    broadcast_in_dim x0 -> x3, local copies, waits for them, and re-layouts: none -> 3.8 us  [the longest x1 1.27 us: whole_body(): second_gain[None]]
  transfers between devices with their start and end apart: 4 -> 0, of which waited for: 4 -> 0; matrix products, arithmetic and copies ran while one was open for 7% -> 0% of each run, Pallas kernels for 0% -> 0%
where the time goes in v1:
time: 61 us; the launch traced here: 60.8 us
  Pallas kernels  54.3 us (89%)
  local copies, waits for them, and re-layouts  6.45 us (11%)
    pallas_call x1, Pallas kernels, whole_body(): pl.pallas_call(functools.partial(kernel, n, heads, picked, stride), out_s...  54.3 us
    unnamed x1, local copies, waits for them, and re-layouts  2.65 us
    broadcast_in_dim x1, local copies, waits for them, and re-layouts, whole_body(): second_gain[None]  1.27 us
    broadcast_in_dim x1, local copies, waits for them, and re-layouts, whole_body(): attn_gain[None]  1.27 us
    broadcast_in_dim x1, local copies, waits for them, and re-layouts, whole_body(): mlp_gain[None]  1.26 us

profile of v1, /device:TPU:0, one launch (start us, length us, event | category | flops | bytes accessed | tf_op | source)
XLA Modules:
  0.0 60.8 jit_solution(14723181340710431296)
XLA Ops:
  0.0 1.3 %broadcast_in_dim.9.gain1_ref = f32[1,768]{1,0:T(1,128)} reshape(f32[768]{0:T(1024)} %param.17) | data formatting | bytes 6144 | tf_op jit(solution)/shard_map/broadcast_in_dim | solution.py:484
  1.3 1.3 %broadcast_in_dim.10.gain_mlp_ref = f32[1,768]{1,0:T(1,128)} reshape(f32[768]{0:T(1024)} %param.22) | data formatting | bytes 6144 | tf_op jit(solution)/shard_map/broadcast_in_dim | solution.py:484
  2.5 1.3 %broadcast_in_dim.11.gain2_ref = f32[1,768]{1,0:T(1,128)} reshape(f32[768]{0:T(1024)} %param.25) | data formatting | bytes 6144 | tf_op jit(solution)/shard_map/broadcast_in_dim | solution.py:484
  3.8 54.3 %encoder.1 = bf16[1024,768]{1,0:T(8,128)(2,1)} custom-call(s32[16]{0:T(128)} %seg_ref.1, s32[16]{0:T(128)} %glob_ref.1, bf16[1024,768]{1,0:T(8,128)(2,1)} %x_ref.1, f32[1,768]{1,0:T(1,128)} %broadcast_in_dim.9.gain1_ref, f32[1,768]{1,0:T(1,128)} %broadcast_in_dim.10.gain_mlp_ref, f32[1,768]{1,0:T(1,128)} %broadcast_in_dim.11.gain2_ref, ...), custom_call_target="tpu_custom_call" | custom-call | tf_op jit(solution)/shard_map/encoder/pallas_call | solution.py:456
  58.1 2.7 %copy.18 = bf16[1024,768]{1,0:T(8,128)(2,1)} copy(bf16[1024,768]{1,0:T(8,128)(2,1)} %encoder.1) | data formatting | bytes 3145728

commit v2 on v1

--- a/solution.py
+++ b/solution.py
@@ -281,7 +281,7 @@
     pick = rows % picked
     target = pick * stride + head_column(seg_ref, heads, picked)
     onehot = (iota((chunk, tokens), 1) == target).astype(F32).astype(BF16)
-    hidden = norm_rows(dot32(onehot, x_ref[...]), gain1_ref[...])
+    hidden = norm_rows(dot32(onehot, x_ref[...]), gain1_ref[...][None, :])
     me = first_gather.me
     loads[0].wait()
     kv1[me, 0:picked, :] = own_heads(hidden, wk1)
@@ -340,7 +340,7 @@
 
     def query_chunk(c, carry):
         at = pl.ds(pl.multiple_of(c * chunk, chunk), chunk)
-        hidden = norm_rows(xp[at, :].astype(F32), gain1_ref[...])
+        hidden = norm_rows(xp[at, :].astype(F32), gain1_ref[...][None, :])
         q[at, :] = dot32(hidden, wq1[...]).astype(BF16)
         return carry
 
@@ -384,14 +384,14 @@
         at = pl.ds(pl.multiple_of(c * chunk, chunk), chunk)
         attend(at)
         first = (xp[at, :].astype(F32) + dot32(mix[...], wo_pad1[...])).astype(BF16)
-        normed = norm_rows(first.astype(F32), gain_mlp_ref[...])
+        normed = norm_rows(first.astype(F32), gain_mlp_ref[...][None, :])
         hidden_units = up.shape[1]
         for start in range(0, hidden_units, width):
             part = dot32(normed, up[:, start:start + width])
             inner[:, start:start + width] = gelu(part).astype(BF16)
         second = (first.astype(F32) + dot32(inner[...], down[...])).astype(BF16)
         xp[at, :] = second
-        hidden_two = norm_rows(second.astype(F32), gain2_ref[...])
+        hidden_two = norm_rows(second.astype(F32), gain2_ref[...][None, :])
         q[at, :] = dot32(hidden_two, wq2[...]).astype(BF16)
 
         @pl.when(c == 0)
@@ -481,7 +481,7 @@
         ),
         name="encoder",
     )(
-        segment_offset, global_offset, tokens, attn_gain[None], mlp_gain[None], second_gain[None],
+        segment_offset, global_offset, tokens, attn_gain, mlp_gain, second_gain,
         query_first, key_first, segment_value, output_first, up_weight, down_weight,
         query_second, key_second, value_second, output_second,
     )

time: 61 us -> 57.2 us (0.938)
  local copies, waits for them, and re-layouts: 6.45 us -> 2.65 us
    broadcast_in_dim x3 -> x0, local copies, waits for them, and re-layouts: 3.8 us -> none  [the longest x1 1.27 us: whole_body(): second_gain[None]]
where the time goes in v2:
time: 57.2 us; the launch traced here: 57 us
  Pallas kernels  54.4 us (95%)
  local copies, waits for them, and re-layouts  2.65 us (5%)
    pallas_call x1, Pallas kernels, whole_body(): pl.pallas_call(functools.partial(kernel, n, heads, picked, stride), out_s...  54.4 us
    unnamed x1, local copies, waits for them, and re-layouts  2.65 us

profile of v2, /device:TPU:0, one launch (start us, length us, event | category | flops | bytes accessed | tf_op | source)
XLA Modules:
  0.0 57.0 jit_solution(13653587115485227200)
XLA Ops:
  0.0 54.4 %encoder.1 = bf16[1024,768]{1,0:T(8,128)(2,1)} custom-call(s32[16]{0:T(128)} %seg_ref.1, s32[16]{0:T(128)} %glob_ref.1, bf16[1024,768]{1,0:T(8,128)(2,1)} %x_ref.1, f32[768]{0:T(1024)} %gain1_ref.1, f32[768]{0:T(1024)} %gain_mlp_ref.1, f32[768]{0:T(1024)} %gain2_ref.1, bf16[768,768]{1,0:T(8,128)(2,1)} %wq1_hbm.1, bf16[768,768]{1,0:T(8,128)(2,1)} %wk1_hbm.1, ...), custom_call_target="tpu_custom_call" | custom-call | tf_op jit(solution)/shard_map/encoder/pallas_call | solution.py:456
  54.4 2.7 %copy.18 = bf16[1024,768]{1,0:T(8,128)(2,1)} copy(bf16[1024,768]{1,0:T(8,128)(2,1)} %encoder.1) | data formatting | bytes 3145728

commit v3 on v2

--- a/solution.py
+++ b/solution.py
@@ -157,6 +157,7 @@
 BF16 = jnp.bfloat16
 WINDOW = 256
 LANES = 128
+VMEM_BYTES = 62 << 20
 
 
 def iota(shape, axis):
@@ -240,11 +241,11 @@
 
 def kernel(
     n, heads, picked, stride,
-    seg_ref, glob_ref, x_ref, gain1_ref, gain_mlp_ref, gain2_ref,
+    seg_ref, glob_ref, gain1_ref, gain_mlp_ref, gain2_ref, x_hbm,
     wq1_hbm, wk1_hbm, wv1_hbm, wo1_hbm, up_hbm, down_hbm, wq2_hbm, wk2_hbm, wv2_hbm, wo2_hbm,
-    out_ref,
-    wq1, wk1, wv1, wo1, up, down, wq2, wk2, wv2, wo2, wo_pad1, wo_pad2,
-    xp, q, kv1, kv2, km, vp, perm, perm_back, mix, inner, sem, ssem1, rsem1, ssem2, rsem2,
+    out_ref, back_ref,
+    x_ref, wq1, wk1, wv1, wo1, up, down, wq2, wk2, wv2, wo2, wo_pad1, wo_pad2,
+    xp, q, kv1, kv2, km, vp, moves, perm, mix, inner, sem, ssem1, rsem1, ssem2, rsem2,
 ):
     tokens, width = x_ref.shape
     size = width // heads
@@ -258,8 +259,10 @@
     pairs = [(wk1_hbm, wk1), (wv1_hbm, wv1), (wq1_hbm, wq1), (wo1_hbm, wo1), (up_hbm, up),
              (down_hbm, down), (wk2_hbm, wk2), (wv2_hbm, wv2), (wq2_hbm, wq2), (wo2_hbm, wo2)]
     loads = [pltpu.make_async_copy(a, b, sem.at[i]) for i, (a, b) in enumerate(pairs)]
-    for load in loads:
-        load.start()
+    tokens_load = pltpu.make_async_copy(x_hbm, x_ref, sem.at[len(pairs)])
+    tokens_load.start()
+    loads[0].start()
+    loads[1].start()
 
     first_gather = Gather(n, kv1, ssem1, rsem1)
     second_gather = Gather(n, kv2, ssem2, rsem2)
@@ -281,11 +284,14 @@
     pick = rows % picked
     target = pick * stride + head_column(seg_ref, heads, picked)
     onehot = (iota((chunk, tokens), 1) == target).astype(F32).astype(BF16)
+    tokens_load.wait()
     hidden = norm_rows(dot32(onehot, x_ref[...]), gain1_ref[...][None, :])
     me = first_gather.me
     loads[0].wait()
     kv1[me, 0:picked, :] = own_heads(hidden, wk1)
     loads[1].wait()
+    for load in loads[2:]:
+        load.start()
     kv1[me, picked:2 * picked, :] = own_heads(hidden, wv1)
     pl.semaphore_wait(barrier, len(peers))
     first_gather.start()
@@ -305,7 +311,7 @@
     rank_row = rank[0:1, :]
     table = jnp.where(same & (rank_row == (a % stride).astype(F32)), 1.0, 0.0)
     perm[...] = table.astype(BF16)
-    perm_back[...] = table.T.astype(BF16)
+    back_ref[...] = table.T.astype(BF16)
     at_head = (iota((chunk, WINDOW), 1) == glob_col)
     head_rank = jnp.sum(jnp.where(at_head, rank_row, 0.0), axis=1, keepdims=True)
     spot = (pick * heads).astype(F32) + head_rank
@@ -326,6 +332,9 @@
         i = h % 2
         ones = iota((keys, LANES), 1) // half == i
         vp[h // 2, i * keys:(i + 1) * keys, LANES:] = jnp.where(ones, 1.0, 0.0).astype(BF16)
+        source = iota((WINDOW, LANES), 0) - (h * size - window_of(h))
+        goal = iota((WINDOW, LANES), 1) - i * half
+        moves[h] = jnp.where((source == goal) & (goal >= 0) & (goal < size), 1.0, 0.0).astype(BF16)
     for source, padded, load in ((wo1, wo_pad1, loads[3]), (wo2, wo_pad2, None)):
         if load is None:
             continue
@@ -338,13 +347,15 @@
 
     loads[2].wait()
 
+    large = 2 * chunk
+
     def query_chunk(c, carry):
-        at = pl.ds(pl.multiple_of(c * chunk, chunk), chunk)
+        at = pl.ds(pl.multiple_of(c * large, large), large)
         hidden = norm_rows(xp[at, :].astype(F32), gain1_ref[...][None, :])
         q[at, :] = dot32(hidden, wq1[...]).astype(BF16)
         return carry
 
-    lax.fori_loop(0, chunks, query_chunk, 0)
+    lax.fori_loop(0, tokens // large, query_chunk, 0)
     first_gather.third()
     first_gather.finish()
 
@@ -356,12 +367,10 @@
             begin = h * size - window_of(h)
             km[h, begin:begin + size, :] = turned[h * size:(h + 1) * size, :]
             i = h % 2
-            c, l = iota((WINDOW, LANES), 0) - begin, iota((WINDOW, LANES), 1) - i * half
-            shift = jnp.where((c == l) & (l >= 0) & (l < size), 1.0, 0.0).astype(BF16)
-            moved = dot32(value[:, window_of(h):window_of(h) + WINDOW], shift)
+            moved = dot32(value[:, window_of(h):window_of(h) + WINDOW], moves[h])
             vp[h // 2, i * keys:(i + 1) * keys, 0:LANES] = moved.astype(BF16)
 
-    def attend(at):
+    def attend(at, count):
         for pair in range(heads // 2):
             parts = []
             for h in (2 * pair, 2 * pair + 1):
@@ -371,47 +380,38 @@
                 parts.append(jnp.exp2((scores - top) * scale).astype(BF16))
             both = dot32(jnp.concatenate(parts, axis=1), vp[pair])
             mixed = both[:, :LANES] / both[:, LANES:]
-            mix[:, pair * LANES:(pair + 1) * LANES] = mixed.astype(BF16)
+            mix[0:count, pair * LANES:(pair + 1) * LANES] = mixed.astype(BF16)
 
     set_keys(kv1)
-    loads[4].wait()
-    loads[5].wait()
-    loads[6].wait()
-    loads[7].wait()
-    loads[8].wait()
-
-    def first_chunk(c, carry):
-        at = pl.ds(pl.multiple_of(c * chunk, chunk), chunk)
-        attend(at)
-        first = (xp[at, :].astype(F32) + dot32(mix[...], wo_pad1[...])).astype(BF16)
-        normed = norm_rows(first.astype(F32), gain_mlp_ref[...][None, :])
-        hidden_units = up.shape[1]
-        for start in range(0, hidden_units, width):
+
+    def first_layer(begin, count, after_attention, after_up):
+        at = slice(begin, begin + count)
+        attend(at, count)
+        first = xp[at, :].astype(F32) + dot32(mix[0:count, :], wo_pad1[...])
+        xp[at, :] = first.astype(BF16)
+        after_attention()
+        normed = norm_rows(xp[at, :].astype(F32), gain_mlp_ref[...][None, :])
+        for start in range(0, up.shape[1], width):
             part = dot32(normed, up[:, start:start + width])
-            inner[:, start:start + width] = gelu(part).astype(BF16)
-        second = (first.astype(F32) + dot32(inner[...], down[...])).astype(BF16)
-        xp[at, :] = second
-        hidden_two = norm_rows(second.astype(F32), gain2_ref[...][None, :])
+            inner[0:count, start:start + width] = gelu(part).astype(BF16)
+        after_up()
+        second = xp[at, :].astype(F32) + dot32(inner[0:count, :], down[...])
+        xp[at, :] = second.astype(BF16)
+        hidden_two = norm_rows(xp[at, :].astype(F32), gain2_ref[...][None, :])
         q[at, :] = dot32(hidden_two, wq2[...]).astype(BF16)
-
-        @pl.when(c == 0)
-        def _():
-            picked_rows = dot32(onehot_two, hidden_two).astype(BF16)
-            kv2[me, 0:picked, :] = own_heads(picked_rows, wk2)
-            kv2[me, picked:2 * picked, :] = own_heads(picked_rows, wv2)
-            second_gather.start()
-
-        @pl.when(c == 1)
-        def _():
-            second_gather.second()
-
-        @pl.when(c == 2)
-        def _():
-            second_gather.third()
-
-        return carry
-
-    lax.fori_loop(0, chunks, first_chunk, 0)
+        return hidden_two
+
+    def wait_for(*which):
+        for i in which:
+            loads[i].wait()
+
+    hidden_two = first_layer(0, chunk, lambda: wait_for(4, 5), lambda: wait_for(6, 7, 8))
+    picked_rows = dot32(onehot_two, hidden_two).astype(BF16)
+    kv2[me, 0:picked, :] = own_heads(picked_rows, wk2)
+    kv2[me, picked:2 * picked, :] = own_heads(picked_rows, wv2)
+    second_gather.start()
+    first_layer(chunk, tokens - chunk, second_gather.second, second_gather.third)
+
     loads[9].wait()
     for h in range(heads):
         wo_pad2[h * half:h * half + size, :] = wo2[h * size:(h + 1) * size, :]
@@ -420,20 +420,22 @@
     set_keys(kv2)
 
     def last_chunk(c, carry):
-        at = pl.ds(pl.multiple_of(c * chunk, chunk), chunk)
-        attend(at)
-        xp[at, :] = (xp[at, :].astype(F32) + dot32(mix[...], wo_pad2[...])).astype(BF16)
+        at = pl.ds(pl.multiple_of(c * large, large), large)
+        attend(at, large)
+        done = xp[at, :].astype(F32) + dot32(mix[0:large, :], wo_pad2[...])
+        done = done.astype(BF16)
+        for i in range(large // chunk):
+            for j in range(picked):
+                row = pl.multiple_of(j * stride + (c * (large // chunk) + i) * heads, heads)
+                block = i * chunk + j * heads
+                out_ref[pl.ds(row, heads), :] = done[block:block + heads]
         return carry
 
-    lax.fori_loop(0, chunks, last_chunk, 0)
-    for g in range(tokens // WINDOW):
-        blocks = []
-        for j in range(group):
-            for c in range(chunks):
-                at = c * chunk + (g * group + j) * heads
-                blocks.append(xp[at:at + heads, :])
-        moved = dot32(perm_back[...], jnp.concatenate(blocks, axis=0))
-        out_ref[g * WINDOW:(g + 1) * WINDOW, :] = moved.astype(BF16)
+    lax.fori_loop(0, tokens // large, last_chunk, 0)
+
+
+def reorder_kernel(back_ref, x_ref, out_ref):
+    out_ref[...] = dot32(back_ref[...], x_ref[...]).astype(BF16)
 
 
 def whole_body(
@@ -453,12 +455,16 @@
     smem = pl.BlockSpec(memory_space=pltpu.SMEM)
     square = pltpu.VMEM((width, width), BF16)
     padded = pltpu.VMEM((heads * LANES // 2, width), BF16)
-    return pl.pallas_call(
+    done, back = pl.pallas_call(
         functools.partial(kernel, n, heads, picked, stride),
-        out_shape=jax.ShapeDtypeStruct(tokens.shape, tokens.dtype),
-        in_specs=[smem, smem, vmem, vmem, vmem, vmem] + [any_space] * 10,
-        out_specs=vmem,
+        out_shape=(
+            jax.ShapeDtypeStruct(tokens.shape, BF16),
+            jax.ShapeDtypeStruct((WINDOW, WINDOW), BF16),
+        ),
+        in_specs=[smem, smem, vmem, vmem, vmem] + [any_space] * 11,
+        out_specs=(vmem, vmem),
         scratch_shapes=[
+            pltpu.VMEM((count, width), BF16),
             square, square, square, square,
             pltpu.VMEM((width, units), BF16), pltpu.VMEM((units, width), BF16),
             square, square, square, square, padded, padded,
@@ -468,23 +474,33 @@
             pltpu.VMEM((n, 2 * picked, width), BF16),
             pltpu.VMEM((heads, WINDOW, KEYS), BF16),
             pltpu.VMEM((heads // 2, 2 * KEYS, 2 * LANES), BF16),
+            pltpu.VMEM((heads, WINDOW, LANES), BF16),
             pltpu.VMEM((WINDOW, WINDOW), BF16),
-            pltpu.VMEM((WINDOW, WINDOW), BF16),
-            pltpu.VMEM((chunk, heads * LANES // 2), BF16),
-            pltpu.VMEM((chunk, units), BF16),
-            pltpu.SemaphoreType.DMA((10,)),
+            pltpu.VMEM((count - chunk, heads * LANES // 2), BF16),
+            pltpu.VMEM((count - chunk, units), BF16),
+            pltpu.SemaphoreType.DMA((11,)),
             pltpu.SemaphoreType.DMA((n,)), pltpu.SemaphoreType.DMA((n,)),
             pltpu.SemaphoreType.DMA((n,)), pltpu.SemaphoreType.DMA((n,)),
         ],
         compiler_params=pltpu.CompilerParams(
-            collective_id=0, has_side_effects=True, vmem_limit_bytes=60 << 20
+            collective_id=0, has_side_effects=True, vmem_limit_bytes=VMEM_BYTES
         ),
         name="encoder",
     )(
-        segment_offset, global_offset, tokens, attn_gain, mlp_gain, second_gain,
+        segment_offset, global_offset, attn_gain, mlp_gain, second_gain, tokens,
         query_first, key_first, segment_value, output_first, up_weight, down_weight,
         query_second, key_second, value_second, output_second,
     )
+    rows = pl.BlockSpec((WINDOW, width), lambda i: (i, 0))
+    return pl.pallas_call(
+        reorder_kernel,
+        grid=(count // WINDOW,),
+        out_shape=jax.ShapeDtypeStruct(tokens.shape, BF16),
+        in_specs=[pl.BlockSpec((WINDOW, WINDOW), lambda i: (0, 0)), rows],
+        out_specs=rows,
+        compiler_params=pltpu.CompilerParams(vmem_limit_bytes=VMEM_BYTES),
+        name="reorder",
+    )(back, done)
 
 
 def fits(mesh):

time: 57.2 us -> 59 us (1.031)
  Pallas kernels: 54.4 us -> 58.8 us
  local copies, waits for them, and re-layouts: 2.65 us -> 0 us
    pallas_call x0 -> x1, Pallas kernels: none -> 4.09 us  [whole_body(): pl.pallas_call(reorder_kernel, grid=(count // WINDOW,), out_shape=jax.Sha...]
    unnamed x1 -> x0, local copies, waits for them, and re-layouts: 2.65 us -> none
where the time goes in v3:
time: 59 us; the launch traced here: 58.8 us
  Pallas kernels  58.8 us (100%)
    pallas_call x1, Pallas kernels, whole_body(): pl.pallas_call(functools.partial(kernel, n, heads, picked, stride), out_s...  54.7 us
    pallas_call x1, Pallas kernels, whole_body(): pl.pallas_call(reorder_kernel, grid=(count // WINDOW,), out_shape=jax.Sha...  4.09 us

profile of v3, /device:TPU:0, one launch (start us, length us, event | category | flops | bytes accessed | tf_op | source)
XLA Modules:
  0.0 58.8 jit_solution(16224837486684333255)
XLA Ops:
  0.0 54.7 %encoder.1 = (bf16[1024,768]{1,0:T(8,128)(2,1)}, bf16[256,256]{1,0:T(8,128)(2,1)}) custom-call(s32[16]{0:T(128)} %seg_ref.1, s32[16]{0:T(128)} %glob_ref.1, f32[768]{0:T(1024)} %gain1_ref.1, f32[768]{0:T(1024)} %gain_mlp_ref.1, f32[768]{0:T(1024)} %gain2_ref.1, bf16[1024,768]{1,0:T(8,128)(2,1)} %x_hbm.1, bf16[768,768]{1,0:T(8,128)(2,1)} %wq1_hbm.1, ...), custom_call_target="tpu_custom_call" | custom-call | tf_op jit(solution)/shard_map/encoder/pallas_call | solution.py:458
  54.7 4.1 %reorder.1 = bf16[1024,768]{1,0:T(8,128)(2,1)} custom-call(bf16[256,256]{1,0:T(8,128)(2,1)} %get-tuple-element.7.back_ref, bf16[1024,768]{1,0:T(8,128)(2,1)} %get-tuple-element.8.x_ref), custom_call_target="tpu_custom_call" | custom-call | tf_op jit(solution)/shard_map/reorder/pallas_call | solution.py:495

commit v4 on v3

--- a/solution.py
+++ b/solution.py
@@ -243,9 +243,9 @@
     n, heads, picked, stride,
     seg_ref, glob_ref, gain1_ref, gain_mlp_ref, gain2_ref, x_hbm,
     wq1_hbm, wk1_hbm, wv1_hbm, wo1_hbm, up_hbm, down_hbm, wq2_hbm, wk2_hbm, wv2_hbm, wo2_hbm,
-    out_ref, back_ref,
+    out_ref,
     x_ref, wq1, wk1, wv1, wo1, up, down, wq2, wk2, wv2, wo2, wo_pad1, wo_pad2,
-    xp, q, kv1, kv2, km, vp, moves, perm, mix, inner, sem, ssem1, rsem1, ssem2, rsem2,
+    xp, q, kv1, kv2, km, vp, moves, perm, perm_back, mix, inner, sem, ssem1, rsem1, ssem2, rsem2,
 ):
     tokens, width = x_ref.shape
     size = width // heads
@@ -290,8 +290,7 @@
     loads[0].wait()
     kv1[me, 0:picked, :] = own_heads(hidden, wk1)
     loads[1].wait()
-    for load in loads[2:]:
-        load.start()
+    loads[2].start()
     kv1[me, picked:2 * picked, :] = own_heads(hidden, wv1)
     pl.semaphore_wait(barrier, len(peers))
     first_gather.start()
@@ -311,7 +310,7 @@
     rank_row = rank[0:1, :]
     table = jnp.where(same & (rank_row == (a % stride).astype(F32)), 1.0, 0.0)
     perm[...] = table.astype(BF16)
-    back_ref[...] = table.T.astype(BF16)
+    perm_back[...] = table.T.astype(BF16)
     at_head = (iota((chunk, WINDOW), 1) == glob_col)
     head_rank = jnp.sum(jnp.where(at_head, rank_row, 0.0), axis=1, keepdims=True)
     spot = (pick * heads).astype(F32) + head_rank
@@ -327,6 +326,20 @@
     def window_of(h):
         return min(h * size // LANES * LANES, width - WINDOW)
 
+    loads[2].wait()
+    for load in loads[3:]:
+        load.start()
+
+    large = 2 * chunk
+
+    def query_chunk(c, carry):
+        at = pl.ds(pl.multiple_of(c * large, large), large)
+        hidden = norm_rows(xp[at, :].astype(F32), gain1_ref[...][None, :])
+        q[at, :] = dot32(hidden, wq1[...]).astype(BF16)
+        return carry
+
+    lax.fori_loop(0, tokens // large, query_chunk, 0)
+    first_gather.second()
     for h in range(heads):
         km[h] = jnp.zeros((WINDOW, keys), BF16)
         i = h % 2
@@ -335,27 +348,6 @@
         source = iota((WINDOW, LANES), 0) - (h * size - window_of(h))
         goal = iota((WINDOW, LANES), 1) - i * half
         moves[h] = jnp.where((source == goal) & (goal >= 0) & (goal < size), 1.0, 0.0).astype(BF16)
-    for source, padded, load in ((wo1, wo_pad1, loads[3]), (wo2, wo_pad2, None)):
-        if load is None:
-            continue
-        load.wait()
-        for h in range(heads):
-            padded[h * half:h * half + size, :] = source[h * size:(h + 1) * size, :]
-            padded[h * half + size:(h + 1) * half, :] = jnp.zeros((half - size, width), BF16)
-
-    first_gather.second()
-
-    loads[2].wait()
-
-    large = 2 * chunk
-
-    def query_chunk(c, carry):
-        at = pl.ds(pl.multiple_of(c * large, large), large)
-        hidden = norm_rows(xp[at, :].astype(F32), gain1_ref[...][None, :])
-        q[at, :] = dot32(hidden, wq1[...]).astype(BF16)
-        return carry
-
-    lax.fori_loop(0, tokens // large, query_chunk, 0)
     first_gather.third()
     first_gather.finish()
 
@@ -382,7 +374,14 @@
             mixed = both[:, :LANES] / both[:, LANES:]
             mix[0:count, pair * LANES:(pair + 1) * LANES] = mixed.astype(BF16)
 
+    def pad_rows(source, padded):
+        for h in range(heads):
+            padded[h * half:h * half + size, :] = source[h * size:(h + 1) * size, :]
+            padded[h * half + size:(h + 1) * half, :] = jnp.zeros((half - size, width), BF16)
+
     set_keys(kv1)
+    loads[3].wait()
+    pad_rows(wo1, wo_pad1)
 
     def first_layer(begin, count, after_attention, after_up):
         at = slice(begin, begin + count)
@@ -413,9 +412,7 @@
     first_layer(chunk, tokens - chunk, second_gather.second, second_gather.third)
 
     loads[9].wait()
-    for h in range(heads):
-        wo_pad2[h * half:h * half + size, :] = wo2[h * size:(h + 1) * size, :]
-        wo_pad2[h * half + size:(h + 1) * half, :] = jnp.zeros((half - size, width), BF16)
+    pad_rows(wo2, wo_pad2)
     second_gather.finish()
     set_keys(kv2)
 
@@ -423,19 +420,18 @@
         at = pl.ds(pl.multiple_of(c * large, large), large)
         attend(at, large)
         done = xp[at, :].astype(F32) + dot32(mix[0:large, :], wo_pad2[...])
-        done = done.astype(BF16)
-        for i in range(large // chunk):
-            for j in range(picked):
-                row = pl.multiple_of(j * stride + (c * (large // chunk) + i) * heads, heads)
-                block = i * chunk + j * heads
-                out_ref[pl.ds(row, heads), :] = done[block:block + heads]
+        xp[at, :] = done.astype(BF16)
         return carry
 
     lax.fori_loop(0, tokens // large, last_chunk, 0)
-
-
-def reorder_kernel(back_ref, x_ref, out_ref):
-    out_ref[...] = dot32(back_ref[...], x_ref[...]).astype(BF16)
+    for g in range(tokens // WINDOW):
+        blocks = []
+        for j in range(group):
+            for c in range(chunks):
+                begin = c * chunk + (g * group + j) * heads
+                blocks.append(xp[begin:begin + heads, :])
+        moved = dot32(perm_back[...], jnp.concatenate(blocks, axis=0))
+        out_ref[g * WINDOW:(g + 1) * WINDOW, :] = moved.astype(BF16)
 
 
 def whole_body(
@@ -455,14 +451,11 @@
     smem = pl.BlockSpec(memory_space=pltpu.SMEM)
     square = pltpu.VMEM((width, width), BF16)
     padded = pltpu.VMEM((heads * LANES // 2, width), BF16)
-    done, back = pl.pallas_call(
+    return pl.pallas_call(
         functools.partial(kernel, n, heads, picked, stride),
-        out_shape=(
-            jax.ShapeDtypeStruct(tokens.shape, BF16),
-            jax.ShapeDtypeStruct((WINDOW, WINDOW), BF16),
-        ),
+        out_shape=jax.ShapeDtypeStruct(tokens.shape, BF16),
         in_specs=[smem, smem, vmem, vmem, vmem] + [any_space] * 11,
-        out_specs=(vmem, vmem),
+        out_specs=vmem,
         scratch_shapes=[
             pltpu.VMEM((count, width), BF16),
             square, square, square, square,
@@ -475,6 +468,7 @@
             pltpu.VMEM((heads, WINDOW, KEYS), BF16),
             pltpu.VMEM((heads // 2, 2 * KEYS, 2 * LANES), BF16),
             pltpu.VMEM((heads, WINDOW, LANES), BF16),
+            pltpu.VMEM((WINDOW, WINDOW), BF16),
             pltpu.VMEM((WINDOW, WINDOW), BF16),
             pltpu.VMEM((count - chunk, heads * LANES // 2), BF16),
             pltpu.VMEM((count - chunk, units), BF16),
@@ -491,16 +485,6 @@
         query_first, key_first, segment_value, output_first, up_weight, down_weight,
         query_second, key_second, value_second, output_second,
     )
-    rows = pl.BlockSpec((WINDOW, width), lambda i: (i, 0))
-    return pl.pallas_call(
-        reorder_kernel,
-        grid=(count // WINDOW,),
-        out_shape=jax.ShapeDtypeStruct(tokens.shape, BF16),
-        in_specs=[pl.BlockSpec((WINDOW, WINDOW), lambda i: (0, 0)), rows],
-        out_specs=rows,
-        compiler_params=pltpu.CompilerParams(vmem_limit_bytes=VMEM_BYTES),
-        name="reorder",
-    )(back, done)
 
 
 def fits(mesh):

time: 59 us -> 57.9 us (0.981)
  Pallas kernels: 58.8 us -> 55 us
  local copies, waits for them, and re-layouts: 0 us -> 2.65 us
    pallas_call x1 -> x0, Pallas kernels: 4.09 us -> none  [whole_body(): pl.pallas_call(reorder_kernel, grid=(count // WINDOW,), out_shape=jax.Sha...]
    unnamed x0 -> x1, local copies, waits for them, and re-layouts: none -> 2.65 us
where the time goes in v4:
time: 57.9 us; the launch traced here: 57.7 us
  Pallas kernels  55 us (95%)
  local copies, waits for them, and re-layouts  2.65 us (5%)
    pallas_call x1, Pallas kernels, whole_body(): pl.pallas_call(functools.partial(kernel, n, heads, picked, stride), out_s...  55 us
    unnamed x1, local copies, waits for them, and re-layouts  2.65 us

profile of v4, /device:TPU:0, one launch (start us, length us, event | category | flops | bytes accessed | tf_op | source)
XLA Modules:
  0.0 57.7 jit_solution(9218015000657553584)
XLA Ops:
  0.0 55.0 %encoder.1 = bf16[1024,768]{1,0:T(8,128)(2,1)} custom-call(s32[16]{0:T(128)} %seg_ref.1, s32[16]{0:T(128)} %glob_ref.1, f32[768]{0:T(1024)} %gain1_ref.1, f32[768]{0:T(1024)} %gain_mlp_ref.1, f32[768]{0:T(1024)} %gain2_ref.1, bf16[1024,768]{1,0:T(8,128)(2,1)} %x_hbm.1, bf16[768,768]{1,0:T(8,128)(2,1)} %wq1_hbm.1, bf16[768,768]{1,0:T(8,128)(2,1)} %wk1_hbm.1, ...), custom_call_target="tpu_custom_call" | custom-call | tf_op jit(solution)/shard_map/encoder/pallas_call | solution.py:454
  55.1 2.7 %copy.18 = bf16[1024,768]{1,0:T(8,128)(2,1)} copy(bf16[1024,768]{1,0:T(8,128)(2,1)} %encoder.1) | data formatting | bytes 3145728
